TPU v7x, 32 devices: a whole 2x2x4 slice. The times are simulated.
32 devices in a mesh: ctx: 8 (over z, x), tp: 4 (over y, core).
Axes of the slice: x: 2, y: 2, z: 4, core: 2. Of those that a mesh axis runs over, the one named last changes fastest.
Arguments:
- hidden_input: bfloat16 [256, 8192], P(None, 'ctx'), may hold values from -6 to 6
- w_query: bfloat16 [8192, 8192], P('ctx', 'tp')
- key_value_weight: bfloat16 [8192, 2, 1024], P('ctx', None, 'tp'), may hold values from -0.0625 to 0.0625
- w_out: bfloat16 [8192, 8192], P('tp', 'ctx'), may hold values from -0.0625 to 0.0625
- key_value_cache: bfloat16 [2, 8, 32768, 128], P(None, 'tp', 'ctx'), may hold values from -6 to 6
- filled: int32 [8], P('ctx'), may hold values from 512 to 4096, as said below
- positions: int32 [256], replicated, may hold values from 0 to 255, each once
Outputs:
- layer_out: bfloat16 [256, 8192], P('tp', 'ctx')
Inputs may be any that keep to these rules, and one draw needn't show every extreme that they name: `filled`: every shard has at least 512 used slots; some shard is full and some holds exactly 512.
All inputs are finite; a program needn't handle non-finite values.
Results may differ from a plain program's by a relative error of at most 0.0045.
The roundings to bfloat16 on the way count: a program that leaves them out, or rounds other values in their place, can miss the bound.
Values may be sent and summed in bfloat16 or wider, within the bound.
A program may use at most 128 MiB of HBM per device.

v0:
```python
import math
import jax
import jax.numpy as jnp
from jax import lax
from jax.sharding import PartitionSpec as P

NEG_FILL = -1e30


def cache_attend(query_rows, key_rows, val_rows, filled_now, inv_root):
    slots = key_rows.shape[1]
    block = math.gcd(slots, 1024)
    blocks = slots // block

    def block_step(block_idx, carry):
        row_max, denom, accum = carry
        key_block = lax.dynamic_slice_in_dim(key_rows, block_idx * block, block, 1)
        val_block = lax.dynamic_slice_in_dim(val_rows, block_idx * block, block, 1)
        scores = (
            jnp.einsum("kgrd,ksd->kgrs", query_rows, key_block, preferred_element_type=jnp.float32)
            * inv_root
        )
        places = block_idx * block + jnp.arange(block, dtype=jnp.int32)
        scores = jnp.where(places < filled_now, scores, NEG_FILL)
        new_max = jnp.maximum(row_max, jnp.max(scores, axis=-1))
        rescale = jnp.exp(row_max - new_max)
        probs = jnp.exp(scores - new_max[..., None])
        update = jnp.einsum(
            "kgrs,ksd->kgrd",
            probs.astype(jnp.bfloat16),
            val_block,
            preferred_element_type=jnp.float32,
        )
        accum = accum * rescale[..., None] + update
        denom = denom * rescale + jnp.sum(probs, axis=-1)
        return (new_max, denom, accum)

    start = (
        jnp.full(query_rows.shape[:3], NEG_FILL, jnp.float32),
        jnp.zeros(query_rows.shape[:3], jnp.float32),
        jnp.zeros(query_rows.shape, jnp.float32),
    )
    row_max, denom, accum = lax.fori_loop(0, blocks, block_step, start)
    return (row_max + jnp.log(denom), accum / denom[..., None])


def block_attend(query_rows, key_rows, val_rows, causal_mask, inv_root):
    scores = (
        jnp.einsum("kgrd,ksd->kgrs", query_rows, key_rows, preferred_element_type=jnp.float32)
        * inv_root
    )
    scores = jnp.where(causal_mask[None, None], scores, NEG_FILL)
    row_max = jnp.max(scores, axis=-1)
    probs = jnp.exp(scores - row_max[..., None])
    denom = jnp.sum(probs, axis=-1)
    accum = jnp.einsum(
        "kgrs,ksd->kgrd", probs.astype(jnp.bfloat16), val_rows, preferred_element_type=jnp.float32
    )
    return (row_max + jnp.log(denom), accum / denom[..., None])


def to_tokens(log_sums, outputs):
    row_count = log_sums.shape[2]
    head_dim = outputs.shape[3]
    return (
        log_sums.reshape(-1, row_count).T,
        jnp.transpose(outputs.reshape(-1, row_count, head_dim), (1, 0, 2)),
    )


def body(hidden_input, w_query, key_value_weight, w_out, key_value_cache, filled, positions):
    tokens = hidden_input.shape[0]
    shards = lax.axis_size("ctx")
    own_rows = tokens // shards
    kv_heads = key_value_cache.shape[1]
    head_dim = key_value_cache.shape[3]
    q_heads = w_query.shape[1] // head_dim
    group_size = q_heads // kv_heads
    width_loc = w_query.shape[0]
    inv_root = 1.0 / math.sqrt(head_dim)
    w_in = jnp.concatenate([w_query, key_value_weight.reshape(width_loc, -1)], axis=1)
    projected_all = lax.psum(
        jnp.dot(hidden_input, w_in, preferred_element_type=jnp.float32), "ctx"
    ).astype(jnp.bfloat16)
    query_cols = q_heads * head_dim
    kv_cols = kv_heads * head_dim
    query_rows = jnp.transpose(
        projected_all[:, :query_cols].reshape(tokens, kv_heads, group_size, head_dim), (1, 2, 0, 3)
    )
    new_keys = jnp.transpose(
        projected_all[:, query_cols : query_cols + kv_cols].reshape(tokens, kv_heads, head_dim),
        (1, 0, 2),
    )
    new_vals = jnp.transpose(
        projected_all[:, query_cols + kv_cols :].reshape(tokens, kv_heads, head_dim), (1, 0, 2)
    )
    cache_log, cache_out = to_tokens(
        *cache_attend(query_rows, key_value_cache[0], key_value_cache[1], filled[0], inv_root)
    )
    log_parts, out_parts = (
        lax.all_to_all(cache_log[None], "ctx", split_axis=1, concat_axis=0, tiled=True),
        lax.all_to_all(cache_out[None], "ctx", split_axis=1, concat_axis=0, tiled=True),
    )
    first_own = lax.axis_index("ctx") * own_rows
    own_queries = lax.dynamic_slice_in_dim(query_rows, first_own, own_rows, 2)
    own_positions = lax.dynamic_slice_in_dim(positions, first_own, own_rows, 0)
    causal_mask = positions[None, :] <= own_positions[:, None]
    new_log, new_out = to_tokens(
        *block_attend(own_queries, new_keys, new_vals, causal_mask, inv_root)
    )
    all_log = jnp.concatenate([log_parts, new_log[None]], axis=0)
    all_out = jnp.concatenate([out_parts, new_out[None]], axis=0)
    top_log = jnp.max(all_log, axis=0)
    shares = jnp.exp(all_log - top_log[None])
    merged = jnp.sum(shares[..., None] * all_out, axis=0) / jnp.sum(shares, axis=0)[..., None]
    attended = merged.astype(jnp.bfloat16).reshape(own_rows, query_cols)
    part_out = jnp.dot(
        lax.all_gather(attended, "ctx", axis=0, tiled=True),
        w_out,
        preferred_element_type=jnp.float32,
    )
    return lax.psum_scatter(part_out, "tp", scatter_dimension=0, tiled=True).astype(jnp.bfloat16)


def solution(mesh):
    placed = (
        P(None, "ctx"),
        P("ctx", "tp"),
        P("ctx", None, "tp"),
        P("tp", "ctx"),
        P(None, "tp", "ctx", None),
        P("ctx"),
        P(),
    )
    return jax.shard_map(
        body, mesh=mesh, in_specs=placed, out_specs=P("tp", "ctx"), check_vma=False
    )
```

profile of v0, /device:TPU:0, one launch (start us, length us, event | category | flops | bytes accessed | tf_op | source)
XLA Modules:
  0.0 340.0 jit_solution(6594446714789034644)
XLA Ops:
  8.1 5.3 %fusion.23 = f32[256,2560]{0,1:T(8,128)} fusion(bf16[256,1024]{1,0:T(8,128)(2,1)S(1)} %copy-done, bf16[1024,512]{1,0:T(8,128)(2,1)S(1)} %bitcast.114, bf16[1024,2048]{1,0:T(8,128)(2,1)} %param.10), kind=kOutput, calls=%fused_computation.28 | convolution fusion | flops 1352663040 | bytes 8388608 | tf_op jit(solution)/shard_map/dot_general | solution.py:83
  13.4 109.1 %all-reduce.1 = bf16[256,2560]{0,1:T(8,128)(2,1)S(1)} all-reduce(f32[256,2560]{0,1:T(8,128)} %fusion.23), channel_id=1, replica_groups=mesh['ctx'=8,'tp'=4] {'ctx'}, use_global_device_ids=true, to_apply=%region_0.0 | all-reduce | flops 655360 | bytes 3932160 | tf_op jit(solution)/shard_map/psum | solution.py:82
  125.1 4.4 %slice_bitcast_fusion = (bf16[2,4096,128]{2,1,0:T(8,128)(2,1)}, bf16[2,4096,128]{2,1,0:T(8,128)(2,1)}) fusion(bf16[2,2,4096,128]{3,2,1,0:T(8,128)(2,1)} %param.13), kind=kLoop, calls=%fused_computation.32 | loop fusion | bytes 8388608 | tf_op jit(solution)/shard_map/squeeze | solution.py:98
  129.5 66.4 %while.18 = (s32[]{:T(128)}, f32[2,8,256]{2,1,0:T(8,128)S(1)}, f32[2,8,256]{2,1,0:T(8,128)S(1)}, f32[2,8,256,128]{3,2,1,0:T(8,128)}, s32[]{:T(128)}, /*index=5*/...) while((s32[]{:T(128)}, f32[2,8,256]{2,1,0:T(8,128)S(1)}, ...), condition=%wide.region_4.5_spmd.clone, body=%wide.region_1.4_spmd.clone.sunk | while | flops 2195216384 | bytes 73666816 | solution.py:43
  130.2 3.8 %bitcast_reduce_fusion.2 = (f32[2,8,256]{2,1,0:T(8,128)S(1)}, f32[2,1024,8,256]{3,1,2,0:T(8,128)S(1)}) fusion(pred[1024]{0:T(1024)(128)(4,1)S(1)} %add_compare_fusion.2, bf16[2,8,256,128]{3,2,1,0:T(8,128)(2,1)S(1)} %get-tuple-element.291, bf16[2,4096,128]{2,1,0:T(8,128)(2,1)} %get-tuple-element.290, s32[]{:T(128)S(6)} %select_n.52), kind=kOutput, calls=%fused_computation.1.clone.1 | convolution fusion | flops 1086320640 | bytes 18367492 | tf_op jit(solution)/shard_map/while/body/eval_jaxpr/kgrd,ksd->kgrs/dot_general | solution.py:20
  134.0 4.1 %fusion.58 = f32[2,8,256]{2,1,0:T(8,128)S(1)} fusion(f32[2,1024,8,256]{3,1,2,0:T(8,128)S(1)} %get-tuple-element.258, f32[2,8,256]{2,1,0:T(8,128)S(1)} %select_maximum_fusion.2, pred[1024]{0:T(1024)(128)(4,1)S(1)} %add_compare_fusion.2), kind=kLoop, calls=%fused_computation.5.clone.1 | loop fusion | flops 16773120 | bytes 16811008 | tf_op jit(solution)/shard_map/while/body/eval_jaxpr/reduce_sum | solution.py:35
  138.1 6.7 %fusion.60 = f32[2,8,256,128]{3,2,1,0:T(8,128)S(1)} fusion(f32[2,8,256,128]{3,2,1,0:T(8,128)S(1)} %copy-done.1, f32[2,1024,8,256]{3,1,2,0:T(8,128)S(1)} %get-tuple-element.258, f32[2,8,256]{2,1,0:T(8,128)S(1)} %select_maximum_fusion.2, pred[1024]{0:T(1024)(128)(4,1)S(1)} %add_compare_fusion.2, f32[2,8,256]{2,1,0:T(8,128)S(1)} %get-tuple-element.260, ...), kind=kOutput, calls=%fused_computation.9.clone.1 | convolution fusion | flops 1092091904 | bytes 21529604 | tf_op jit(solution)/shard_map/while/body/eval_jaxpr/kgrs,ksd->kgrd/dot_general | solution.py:28
  146.8 3.8 %bitcast_reduce_fusion.2 = (f32[2,8,256]{2,1,0:T(8,128)S(1)}, f32[2,1024,8,256]{3,1,2,0:T(8,128)S(1)}) fusion(pred[1024]{0:T(1024)(128)(4,1)S(1)} %add_compare_fusion.2, bf16[2,8,256,128]{3,2,1,0:T(8,128)(2,1)S(1)} %get-tuple-element.291, bf16[2,4096,128]{2,1,0:T(8,128)(2,1)} %get-tuple-element.290, s32[]{:T(128)S(6)} %select_n.52), kind=kOutput, calls=%fused_computation.1.clone.1 | convolution fusion | flops 1086320640 | bytes 18367492 | tf_op jit(solution)/shard_map/while/body/eval_jaxpr/kgrd,ksd->kgrs/dot_general | solution.py:20
  150.6 4.1 %fusion.58 = f32[2,8,256]{2,1,0:T(8,128)S(1)} fusion(f32[2,1024,8,256]{3,1,2,0:T(8,128)S(1)} %get-tuple-element.258, f32[2,8,256]{2,1,0:T(8,128)S(1)} %select_maximum_fusion.2, pred[1024]{0:T(1024)(128)(4,1)S(1)} %add_compare_fusion.2), kind=kLoop, calls=%fused_computation.5.clone.1 | loop fusion | flops 16773120 | bytes 16811008 | tf_op jit(solution)/shard_map/while/body/eval_jaxpr/reduce_sum | solution.py:35
  154.7 6.7 %fusion.60 = f32[2,8,256,128]{3,2,1,0:T(8,128)S(1)} fusion(f32[2,8,256,128]{3,2,1,0:T(8,128)S(1)} %copy-done.1, f32[2,1024,8,256]{3,1,2,0:T(8,128)S(1)} %get-tuple-element.258, f32[2,8,256]{2,1,0:T(8,128)S(1)} %select_maximum_fusion.2, pred[1024]{0:T(1024)(128)(4,1)S(1)} %add_compare_fusion.2, f32[2,8,256]{2,1,0:T(8,128)S(1)} %get-tuple-element.260, ...), kind=kOutput, calls=%fused_computation.9.clone.1 | convolution fusion | flops 1092091904 | bytes 21529604 | tf_op jit(solution)/shard_map/while/body/eval_jaxpr/kgrs,ksd->kgrd/dot_general | solution.py:28
  163.4 3.8 %bitcast_reduce_fusion.2 = (f32[2,8,256]{2,1,0:T(8,128)S(1)}, f32[2,1024,8,256]{3,1,2,0:T(8,128)S(1)}) fusion(pred[1024]{0:T(1024)(128)(4,1)S(1)} %add_compare_fusion.2, bf16[2,8,256,128]{3,2,1,0:T(8,128)(2,1)S(1)} %get-tuple-element.291, bf16[2,4096,128]{2,1,0:T(8,128)(2,1)} %get-tuple-element.290, s32[]{:T(128)S(6)} %select_n.52), kind=kOutput, calls=%fused_computation.1.clone.1 | convolution fusion | flops 1086320640 | bytes 18367492 | tf_op jit(solution)/shard_map/while/body/eval_jaxpr/kgrd,ksd->kgrs/dot_general | solution.py:20
  167.2 4.1 %fusion.58 = f32[2,8,256]{2,1,0:T(8,128)S(1)} fusion(f32[2,1024,8,256]{3,1,2,0:T(8,128)S(1)} %get-tuple-element.258, f32[2,8,256]{2,1,0:T(8,128)S(1)} %select_maximum_fusion.2, pred[1024]{0:T(1024)(128)(4,1)S(1)} %add_compare_fusion.2), kind=kLoop, calls=%fused_computation.5.clone.1 | loop fusion | flops 16773120 | bytes 16811008 | tf_op jit(solution)/shard_map/while/body/eval_jaxpr/reduce_sum | solution.py:35
  171.3 6.7 %fusion.60 = f32[2,8,256,128]{3,2,1,0:T(8,128)S(1)} fusion(f32[2,8,256,128]{3,2,1,0:T(8,128)S(1)} %copy-done.1, f32[2,1024,8,256]{3,1,2,0:T(8,128)S(1)} %get-tuple-element.258, f32[2,8,256]{2,1,0:T(8,128)S(1)} %select_maximum_fusion.2, pred[1024]{0:T(1024)(128)(4,1)S(1)} %add_compare_fusion.2, f32[2,8,256]{2,1,0:T(8,128)S(1)} %get-tuple-element.260, ...), kind=kOutput, calls=%fused_computation.9.clone.1 | convolution fusion | flops 1092091904 | bytes 21529604 | tf_op jit(solution)/shard_map/while/body/eval_jaxpr/kgrs,ksd->kgrd/dot_general | solution.py:28
  180.0 3.8 %bitcast_reduce_fusion.2 = (f32[2,8,256]{2,1,0:T(8,128)S(1)}, f32[2,1024,8,256]{3,1,2,0:T(8,128)S(1)}) fusion(pred[1024]{0:T(1024)(128)(4,1)S(1)} %add_compare_fusion.2, bf16[2,8,256,128]{3,2,1,0:T(8,128)(2,1)S(1)} %get-tuple-element.291, bf16[2,4096,128]{2,1,0:T(8,128)(2,1)} %get-tuple-element.290, s32[]{:T(128)S(6)} %select_n.52), kind=kOutput, calls=%fused_computation.1.clone.1 | convolution fusion | flops 1086320640 | bytes 18367492 | tf_op jit(solution)/shard_map/while/body/eval_jaxpr/kgrd,ksd->kgrs/dot_general | solution.py:20
  183.8 4.1 %fusion.58 = f32[2,8,256]{2,1,0:T(8,128)S(1)} fusion(f32[2,1024,8,256]{3,1,2,0:T(8,128)S(1)} %get-tuple-element.258, f32[2,8,256]{2,1,0:T(8,128)S(1)} %select_maximum_fusion.2, pred[1024]{0:T(1024)(128)(4,1)S(1)} %add_compare_fusion.2), kind=kLoop, calls=%fused_computation.5.clone.1 | loop fusion | flops 16773120 | bytes 16811008 | tf_op jit(solution)/shard_map/while/body/eval_jaxpr/reduce_sum | solution.py:35
  187.9 6.7 %fusion.60 = f32[2,8,256,128]{3,2,1,0:T(8,128)S(1)} fusion(f32[2,8,256,128]{3,2,1,0:T(8,128)S(1)} %copy-done.1, f32[2,1024,8,256]{3,1,2,0:T(8,128)S(1)} %get-tuple-element.258, f32[2,8,256]{2,1,0:T(8,128)S(1)} %select_maximum_fusion.2, pred[1024]{0:T(1024)(128)(4,1)S(1)} %add_compare_fusion.2, f32[2,8,256]{2,1,0:T(8,128)S(1)} %get-tuple-element.260, ...), kind=kOutput, calls=%fused_computation.9.clone.1 | convolution fusion | flops 1092091904 | bytes 21529604 | tf_op jit(solution)/shard_map/while/body/eval_jaxpr/kgrs,ksd->kgrd/dot_general | solution.py:28
  198.2 3.5 %all-to-all-start = ((f32[8,1,512]{2,1,0:T(1,128)}), f32[8,1,512]{2,1,0:T(1,128)S(1)}, u32[]{:S(2)}, u32[]{:S(2)}) async-start(f32[8,1,512]{2,1,0:T(1,128)} %reshape.106), calls=%async_computation | async-start | bytes 32768 | tf_op jit(solution)/shard_map/all_to_all | solution.py:101
  203.6 2.5 copy.69
  208.3 4.3 %all-to-all-start.1 = ((f32[1,256,16,128]{3,2,0,1:T(8,128)}), f32[1,256,16,128]{3,2,0,1:T(8,128)}, u32[]{:S(2)}, u32[]{:S(2)}) async-start(f32[1,256,16,128]{3,2,0,1:T(8,128)} %bitcast.109), calls=%async_computation.1 | async-start | bytes 4194304 | tf_op jit(solution)/shard_map/all_to_all | solution.py:102
  215.3 44.4 %all-to-all-done.1 = f32[1,256,16,128]{3,2,0,1:T(8,128)} async-done(((f32[1,256,16,128]{3,2,0,1:T(8,128)}), f32[1,256,16,128]{3,2,0,1:T(8,128)}, u32[]{:S(2)}, u32[]{:S(2)}) %all-to-all-start.1) | async-done | bytes 2097184 | tf_op jit(solution)/shard_map/all_to_all | solution.py:102
  259.6 2.3 copy.58
  263.6 39.3 %all-gather.2.cloned.1.call-done = bf16[256,2048]{1,0:T(8,128)(2,1)} async-done(((bf16[32,2048]{1,0:T(8,128)(2,1)}), bf16[256,2048]{1,0:T(8,128)(2,1)}) %all-gather.2.cloned.1.call-update) | async-done | bytes 1048592 | tf_op jit(solution)/shard_map/all_gather | solution.py:118
  302.9 4.8 %fusion.43 = f32[256,1024]{1,0:T(8,128)} fusion(bf16[256,2048]{1,0:T(8,128)(2,1)} %all-gather.2.cloned.1.call-done, bf16[2048,1024]{1,0:T(8,128)(2,1)} %param.12), kind=kOutput, calls=%fused_computation.60 | convolution fusion | flops 1073741824 | bytes 6291456 | tf_op jit(solution)/shard_map/dot_general | solution.py:117
  307.7 23.8 %reduce-scatter.2.cloned.1.call-done = f32[64,1024]{1,0:T(8,128)} async-done(((f32[256,1024]{1,0:T(8,128)}), f32[64,1024]{1,0:T(8,128)}) %reduce-scatter.2.cloned.1.call-update) | async-done | bytes 262160 | tf_op jit(solution)/shard_map/reduce_scatter | solution.py:122
  (74 shorter events, 24.3 us)
Async XLA Ops:
  6.5 1.5 copy-start
  134.0 4.1 %copy-start.1 = (f32[2,8,256,128]{3,2,1,0:T(8,128)S(1)}, f32[2,8,256,128]{3,2,1,0:T(8,128)}, u32[]{:S(2)}) copy-start(f32[2,8,256,128]{3,2,1,0:T(8,128)} %get-tuple-element.276) | copy-start | bytes 6291460 | tf_op jit(solution)/shard_map/while
  144.8 1.3 copy-start.2
  150.6 4.1 %copy-start.1 = (f32[2,8,256,128]{3,2,1,0:T(8,128)S(1)}, f32[2,8,256,128]{3,2,1,0:T(8,128)}, u32[]{:S(2)}) copy-start(f32[2,8,256,128]{3,2,1,0:T(8,128)} %get-tuple-element.276) | copy-start | bytes 6291460 | tf_op jit(solution)/shard_map/while
  161.4 1.3 copy-start.2
  167.2 4.1 %copy-start.1 = (f32[2,8,256,128]{3,2,1,0:T(8,128)S(1)}, f32[2,8,256,128]{3,2,1,0:T(8,128)}, u32[]{:S(2)}) copy-start(f32[2,8,256,128]{3,2,1,0:T(8,128)} %get-tuple-element.276) | copy-start | bytes 6291460 | tf_op jit(solution)/shard_map/while
  178.0 1.3 copy-start.2
  183.8 4.1 %copy-start.1 = (f32[2,8,256,128]{3,2,1,0:T(8,128)S(1)}, f32[2,8,256,128]{3,2,1,0:T(8,128)}, u32[]{:S(2)}) copy-start(f32[2,8,256,128]{3,2,1,0:T(8,128)} %get-tuple-element.276) | copy-start | bytes 6291460 | tf_op jit(solution)/shard_map/while
  194.6 1.3 copy-start.2
  198.2 10.1 %all-to-all-start = ((f32[8,1,512]{2,1,0:T(1,128)}), f32[8,1,512]{2,1,0:T(1,128)S(1)}, u32[]{:S(2)}, u32[]{:S(2)}) async-start(f32[8,1,512]{2,1,0:T(1,128)} %reshape.106), calls=%async_computation | async-start | bytes 32768 | tf_op jit(solution)/shard_map/all_to_all | solution.py:101
  203.6 9.3 %copy-start.3 = (s32[256]{0:T(256)S(1)}, s32[256]{0:T(256)}, u32[]{:S(2)}) copy-start(s32[256]{0:T(256)} %param.15) | copy-start | bytes 3076
  208.3 51.4 %all-to-all-start.1 = ((f32[1,256,16,128]{3,2,0,1:T(8,128)}), f32[1,256,16,128]{3,2,0,1:T(8,128)}, u32[]{:S(2)}, u32[]{:S(2)}) async-start(f32[1,256,16,128]{3,2,0,1:T(8,128)} %bitcast.109), calls=%async_computation.1 | async-start | bytes 4194304 | tf_op jit(solution)/shard_map/all_to_all | solution.py:102
  212.6 90.3 %all-gather.2.cloned.1.call-start = ((), (), s32[]{:S(2)}) async-start(), calls=%async_computation.3 | async-start | bytes 1179648 | tf_op jit(solution)/shard_map/all_gather | solution.py:118
  263.5 68.0 %reduce-scatter.2.cloned.1.call-start = ((), (), s32[]{:S(2)}) async-start(), calls=%async_computation.4 | async-start | bytes 1310720 | tf_op jit(solution)/shard_map/reduce_scatter | solution.py:122
Sparse Core Ops, SparseCore 0:
  263.7 39.2 all-gather.1
  307.8 23.6 reduce-scatter.1
where the time goes:
time: 341 us; the launch traced here: 340 us
  waiting for transfers between devices  110 us (32%)
  blocking collectives  109 us (32%)
  matrix products  52.4 us (15%)
  other arithmetic  26.1 us (8%)
  local copies, waits for them, and re-layouts  20.9 us (6%)
  between operations  13.6 us (4%)
  starting transfers between devices  7.95 us (2%)
    psum x1, blocking collectives, body(): lax.psum(jnp.dot(hidden_input, w_in, preferred_element_type=jnp.float32),...  109 us
    all_to_all x1, waiting for transfers between devices, body(): lax.all_to_all(cache_out[None], 'ctx', split_axis=1, concat_axis=0, tiled...  44.4 us
    all_gather x1, waiting for transfers between devices, body(): lax.all_gather(attended, 'ctx', axis=0, tiled=True)  39.3 us
    dot_general x4, matrix products, block_step(): jnp.einsum('kgrs,ksd->kgrd', probs.astype(jnp.bfloat16), val_block, prefe...  26.7 us
    reduce_scatter x1, waiting for transfers between devices, body(): lax.psum_scatter(part_out, 'tp', scatter_dimension=0, tiled=True)  23.8 us
    reduce_sum x4, other arithmetic, block_step(): denom = denom * rescale + jnp.sum(probs, axis=-1)  16.3 us
    dot_general x4, matrix products, block_step(): jnp.einsum('kgrd,ksd->kgrs', query_rows, key_block, preferred_element_typ...  15.1 us
  transfers between devices with their start and end apart: 4, of which 4 were waited for; matrix products, arithmetic and copies ran while one was open for 2% of the time, Pallas kernels for 0%

commit v1 on v0

--- a/solution.py
+++ b/solution.py
@@ -5,6 +5,18 @@
 from jax.sharding import PartitionSpec as P
 
 NEG_FILL = -1e30
+
+
+def gather_by_bits(x, axis, dim):
+    ways, here, turn = (lax.axis_size(axis), lax.axis_index(axis), x.shape[dim])
+    line, have = (x, 1)
+    while have < ways:
+        line = jnp.concatenate(
+            [line, lax.ppermute(line, axis, [(d, (d - have) % ways) for d in range(ways)])],
+            axis=dim,
+        )
+        have = 2 * have
+    return jnp.roll(line, here * turn, axis=dim)
 
 
 def cache_attend(query_rows, key_rows, val_rows, filled_now, inv_root):
@@ -115,9 +127,7 @@
     merged = jnp.sum(shares[..., None] * all_out, axis=0) / jnp.sum(shares, axis=0)[..., None]
     attended = merged.astype(jnp.bfloat16).reshape(own_rows, query_cols)
     part_out = jnp.dot(
-        lax.all_gather(attended, "ctx", axis=0, tiled=True),
-        w_out,
-        preferred_element_type=jnp.float32,
+        gather_by_bits(attended, "ctx", 0), w_out, preferred_element_type=jnp.float32
     )
     return lax.psum_scatter(part_out, "tp", scatter_dimension=0, tiled=True).astype(jnp.bfloat16)
 

time: 341 us -> 339 us (level)
  starting transfers between devices: 7.95 us -> 12.2 us
  waiting for transfers between devices: 110 us -> 106 us
    all_gather x1 -> x0, waiting for transfers between devices: 39.3 us -> none  [body(): lax.all_gather(attended, 'ctx', axis=0, tiled=True)]
    ppermute x0 -> x3, waiting for transfers between devices: none -> 32.7 us  [gather_by_bits(): lax.ppermute(line, axis, [(d, (d - have) % ways) for d in range(ways)])]
    ppermute x0 -> x3, starting transfers between devices: none -> 4.14 us  [gather_by_bits(): lax.ppermute(line, axis, [(d, (d - have) % ways) for d in range(ways)])]
  transfers between devices with their start and end apart: 4 -> 6, of which waited for: 4 -> 6; matrix products, arithmetic and copies ran while one was open for 2% -> 2% of each run, Pallas kernels for 0% -> 0%
where the time goes in v1:
time: 339 us; the launch traced here: 338 us
  blocking collectives  109 us (32%)
  waiting for transfers between devices  106 us (31%)
  matrix products  49.9 us (15%)
  other arithmetic  25.8 us (8%)
  local copies, waits for them, and re-layouts  21 us (6%)
  between operations  13.7 us (4%)
  starting transfers between devices  12.2 us (4%)
    psum x1, blocking collectives, body(): lax.psum(jnp.dot(hidden_input, w_in, preferred_element_type=jnp.float32),...  109 us
    all_to_all x1, waiting for transfers between devices, body(): lax.all_to_all(cache_out[None], 'ctx', split_axis=1, concat_axis=0, tiled...  44.3 us
    ppermute x3, waiting for transfers between devices, gather_by_bits(): lax.ppermute(line, axis, [(d, (d - have) % ways) for d in range(ways)])  32.7 us
    reduce_scatter x1, waiting for transfers between devices, body(): lax.psum_scatter(part_out, 'tp', scatter_dimension=0, tiled=True)  26.9 us
    dot_general x4, matrix products, block_step(): jnp.einsum('kgrs,ksd->kgrd', probs.astype(jnp.bfloat16), val_block, prefe...  26.7 us
    reduce_sum x4, other arithmetic, block_step(): denom = denom * rescale + jnp.sum(probs, axis=-1)  16.3 us
    dot_general x4, matrix products, block_step(): jnp.einsum('kgrd,ksd->kgrs', query_rows, key_block, preferred_element_typ...  15.1 us
  transfers between devices with their start and end apart: 6, of which 6 were waited for; matrix products, arithmetic and copies ran while one was open for 2% of the time, Pallas kernels for 0%

profile of v1, /device:TPU:0, one launch (start us, length us, event | category | flops | bytes accessed | tf_op | source)
XLA Modules:
  0.0 338.1 jit_solution(17550801999106035414)
XLA Ops:
  8.1 5.3 %fusion.23 = f32[256,2560]{0,1:T(8,128)} fusion(bf16[256,1024]{1,0:T(8,128)(2,1)S(1)} %copy-done, bf16[1024,512]{1,0:T(8,128)(2,1)S(1)} %bitcast.119, bf16[1024,2048]{1,0:T(8,128)(2,1)} %param.10), kind=kOutput, calls=%fused_computation.28 | convolution fusion | flops 1352663040 | bytes 8388608 | tf_op jit(solution)/shard_map/dot_general | solution.py:95
  13.4 109.1 %all-reduce.1 = bf16[256,2560]{0,1:T(8,128)(2,1)S(1)} all-reduce(f32[256,2560]{0,1:T(8,128)} %fusion.23), channel_id=1, replica_groups=mesh['ctx'=8,'tp'=4] {'ctx'}, use_global_device_ids=true, to_apply=%region_0.0 | all-reduce | flops 655360 | bytes 3932160 | tf_op jit(solution)/shard_map/psum | solution.py:94
  125.1 4.4 %slice_bitcast_fusion = (bf16[2,4096,128]{2,1,0:T(8,128)(2,1)}, bf16[2,4096,128]{2,1,0:T(8,128)(2,1)}) fusion(bf16[2,2,4096,128]{3,2,1,0:T(8,128)(2,1)} %param.13), kind=kLoop, calls=%fused_computation.32 | loop fusion | bytes 8388608 | tf_op jit(solution)/shard_map/squeeze | solution.py:110
  129.5 66.4 %while.18 = (s32[]{:T(128)}, f32[2,8,256]{2,1,0:T(8,128)S(1)}, f32[2,8,256]{2,1,0:T(8,128)S(1)}, f32[2,8,256,128]{3,2,1,0:T(8,128)}, s32[]{:T(128)}, /*index=5*/...) while((s32[]{:T(128)}, f32[2,8,256]{2,1,0:T(8,128)S(1)}, ...), condition=%wide.region_4.5_spmd.clone, body=%wide.region_1.4_spmd.clone.sunk | while | flops 2195216384 | bytes 73666816 | solution.py:55
  130.2 3.8 %bitcast_reduce_fusion.2 = (f32[2,8,256]{2,1,0:T(8,128)S(1)}, f32[2,1024,8,256]{3,1,2,0:T(8,128)S(1)}) fusion(pred[1024]{0:T(1024)(128)(4,1)S(1)} %add_compare_fusion.2, bf16[2,8,256,128]{3,2,1,0:T(8,128)(2,1)S(1)} %get-tuple-element.291, bf16[2,4096,128]{2,1,0:T(8,128)(2,1)} %get-tuple-element.290, s32[]{:T(128)S(6)} %select_n.67), kind=kOutput, calls=%fused_computation.1.clone.1 | convolution fusion | flops 1086320640 | bytes 18367492 | tf_op jit(solution)/shard_map/while/body/eval_jaxpr/kgrd,ksd->kgrs/dot_general | solution.py:32
  134.0 4.1 %fusion.61 = f32[2,8,256]{2,1,0:T(8,128)S(1)} fusion(f32[2,1024,8,256]{3,1,2,0:T(8,128)S(1)} %get-tuple-element.258, f32[2,8,256]{2,1,0:T(8,128)S(1)} %select_maximum_fusion.2, pred[1024]{0:T(1024)(128)(4,1)S(1)} %add_compare_fusion.2), kind=kLoop, calls=%fused_computation.5.clone.1 | loop fusion | flops 16773120 | bytes 16811008 | tf_op jit(solution)/shard_map/while/body/eval_jaxpr/reduce_sum | solution.py:47
  138.1 6.7 %fusion.63 = f32[2,8,256,128]{3,2,1,0:T(8,128)S(1)} fusion(f32[2,8,256,128]{3,2,1,0:T(8,128)S(1)} %copy-done.1, f32[2,1024,8,256]{3,1,2,0:T(8,128)S(1)} %get-tuple-element.258, f32[2,8,256]{2,1,0:T(8,128)S(1)} %select_maximum_fusion.2, pred[1024]{0:T(1024)(128)(4,1)S(1)} %add_compare_fusion.2, f32[2,8,256]{2,1,0:T(8,128)S(1)} %get-tuple-element.260, ...), kind=kOutput, calls=%fused_computation.9.clone.1 | convolution fusion | flops 1092091904 | bytes 21529604 | tf_op jit(solution)/shard_map/while/body/eval_jaxpr/kgrs,ksd->kgrd/dot_general | solution.py:40
  146.8 3.8 %bitcast_reduce_fusion.2 = (f32[2,8,256]{2,1,0:T(8,128)S(1)}, f32[2,1024,8,256]{3,1,2,0:T(8,128)S(1)}) fusion(pred[1024]{0:T(1024)(128)(4,1)S(1)} %add_compare_fusion.2, bf16[2,8,256,128]{3,2,1,0:T(8,128)(2,1)S(1)} %get-tuple-element.291, bf16[2,4096,128]{2,1,0:T(8,128)(2,1)} %get-tuple-element.290, s32[]{:T(128)S(6)} %select_n.67), kind=kOutput, calls=%fused_computation.1.clone.1 | convolution fusion | flops 1086320640 | bytes 18367492 | tf_op jit(solution)/shard_map/while/body/eval_jaxpr/kgrd,ksd->kgrs/dot_general | solution.py:32
  150.6 4.1 %fusion.61 = f32[2,8,256]{2,1,0:T(8,128)S(1)} fusion(f32[2,1024,8,256]{3,1,2,0:T(8,128)S(1)} %get-tuple-element.258, f32[2,8,256]{2,1,0:T(8,128)S(1)} %select_maximum_fusion.2, pred[1024]{0:T(1024)(128)(4,1)S(1)} %add_compare_fusion.2), kind=kLoop, calls=%fused_computation.5.clone.1 | loop fusion | flops 16773120 | bytes 16811008 | tf_op jit(solution)/shard_map/while/body/eval_jaxpr/reduce_sum | solution.py:47
  154.7 6.7 %fusion.63 = f32[2,8,256,128]{3,2,1,0:T(8,128)S(1)} fusion(f32[2,8,256,128]{3,2,1,0:T(8,128)S(1)} %copy-done.1, f32[2,1024,8,256]{3,1,2,0:T(8,128)S(1)} %get-tuple-element.258, f32[2,8,256]{2,1,0:T(8,128)S(1)} %select_maximum_fusion.2, pred[1024]{0:T(1024)(128)(4,1)S(1)} %add_compare_fusion.2, f32[2,8,256]{2,1,0:T(8,128)S(1)} %get-tuple-element.260, ...), kind=kOutput, calls=%fused_computation.9.clone.1 | convolution fusion | flops 1092091904 | bytes 21529604 | tf_op jit(solution)/shard_map/while/body/eval_jaxpr/kgrs,ksd->kgrd/dot_general | solution.py:40
  163.4 3.8 %bitcast_reduce_fusion.2 = (f32[2,8,256]{2,1,0:T(8,128)S(1)}, f32[2,1024,8,256]{3,1,2,0:T(8,128)S(1)}) fusion(pred[1024]{0:T(1024)(128)(4,1)S(1)} %add_compare_fusion.2, bf16[2,8,256,128]{3,2,1,0:T(8,128)(2,1)S(1)} %get-tuple-element.291, bf16[2,4096,128]{2,1,0:T(8,128)(2,1)} %get-tuple-element.290, s32[]{:T(128)S(6)} %select_n.67), kind=kOutput, calls=%fused_computation.1.clone.1 | convolution fusion | flops 1086320640 | bytes 18367492 | tf_op jit(solution)/shard_map/while/body/eval_jaxpr/kgrd,ksd->kgrs/dot_general | solution.py:32
  167.2 4.1 %fusion.61 = f32[2,8,256]{2,1,0:T(8,128)S(1)} fusion(f32[2,1024,8,256]{3,1,2,0:T(8,128)S(1)} %get-tuple-element.258, f32[2,8,256]{2,1,0:T(8,128)S(1)} %select_maximum_fusion.2, pred[1024]{0:T(1024)(128)(4,1)S(1)} %add_compare_fusion.2), kind=kLoop, calls=%fused_computation.5.clone.1 | loop fusion | flops 16773120 | bytes 16811008 | tf_op jit(solution)/shard_map/while/body/eval_jaxpr/reduce_sum | solution.py:47
  171.3 6.7 %fusion.63 = f32[2,8,256,128]{3,2,1,0:T(8,128)S(1)} fusion(f32[2,8,256,128]{3,2,1,0:T(8,128)S(1)} %copy-done.1, f32[2,1024,8,256]{3,1,2,0:T(8,128)S(1)} %get-tuple-element.258, f32[2,8,256]{2,1,0:T(8,128)S(1)} %select_maximum_fusion.2, pred[1024]{0:T(1024)(128)(4,1)S(1)} %add_compare_fusion.2, f32[2,8,256]{2,1,0:T(8,128)S(1)} %get-tuple-element.260, ...), kind=kOutput, calls=%fused_computation.9.clone.1 | convolution fusion | flops 1092091904 | bytes 21529604 | tf_op jit(solution)/shard_map/while/body/eval_jaxpr/kgrs,ksd->kgrd/dot_general | solution.py:40
  180.0 3.8 %bitcast_reduce_fusion.2 = (f32[2,8,256]{2,1,0:T(8,128)S(1)}, f32[2,1024,8,256]{3,1,2,0:T(8,128)S(1)}) fusion(pred[1024]{0:T(1024)(128)(4,1)S(1)} %add_compare_fusion.2, bf16[2,8,256,128]{3,2,1,0:T(8,128)(2,1)S(1)} %get-tuple-element.291, bf16[2,4096,128]{2,1,0:T(8,128)(2,1)} %get-tuple-element.290, s32[]{:T(128)S(6)} %select_n.67), kind=kOutput, calls=%fused_computation.1.clone.1 | convolution fusion | flops 1086320640 | bytes 18367492 | tf_op jit(solution)/shard_map/while/body/eval_jaxpr/kgrd,ksd->kgrs/dot_general | solution.py:32
  183.8 4.1 %fusion.61 = f32[2,8,256]{2,1,0:T(8,128)S(1)} fusion(f32[2,1024,8,256]{3,1,2,0:T(8,128)S(1)} %get-tuple-element.258, f32[2,8,256]{2,1,0:T(8,128)S(1)} %select_maximum_fusion.2, pred[1024]{0:T(1024)(128)(4,1)S(1)} %add_compare_fusion.2), kind=kLoop, calls=%fused_computation.5.clone.1 | loop fusion | flops 16773120 | bytes 16811008 | tf_op jit(solution)/shard_map/while/body/eval_jaxpr/reduce_sum | solution.py:47
  187.9 6.7 %fusion.63 = f32[2,8,256,128]{3,2,1,0:T(8,128)S(1)} fusion(f32[2,8,256,128]{3,2,1,0:T(8,128)S(1)} %copy-done.1, f32[2,1024,8,256]{3,1,2,0:T(8,128)S(1)} %get-tuple-element.258, f32[2,8,256]{2,1,0:T(8,128)S(1)} %select_maximum_fusion.2, pred[1024]{0:T(1024)(128)(4,1)S(1)} %add_compare_fusion.2, f32[2,8,256]{2,1,0:T(8,128)S(1)} %get-tuple-element.260, ...), kind=kOutput, calls=%fused_computation.9.clone.1 | convolution fusion | flops 1092091904 | bytes 21529604 | tf_op jit(solution)/shard_map/while/body/eval_jaxpr/kgrs,ksd->kgrd/dot_general | solution.py:40
  198.2 3.5 %all-to-all-start = ((f32[8,1,512]{2,1,0:T(1,128)}), f32[8,1,512]{2,1,0:T(1,128)S(1)}, u32[]{:S(2)}, u32[]{:S(2)}) async-start(f32[8,1,512]{2,1,0:T(1,128)} %reshape.106), calls=%async_computation | async-start | bytes 32768 | tf_op jit(solution)/shard_map/all_to_all | solution.py:113
  203.6 2.5 copy.73
  208.3 4.5 %all-to-all-start.1 = ((f32[1,256,16,128]{3,2,0,1:T(8,128)}), f32[1,256,16,128]{3,2,0,1:T(8,128)}, u32[]{:S(2)}, u32[]{:S(2)}) async-start(f32[1,256,16,128]{3,2,0,1:T(8,128)} %bitcast.114), calls=%async_computation.1 | async-start | bytes 4194304 | tf_op jit(solution)/shard_map/all_to_all | solution.py:114
  215.4 44.3 %all-to-all-done.1 = f32[1,256,16,128]{3,2,0,1:T(8,128)} async-done(((f32[1,256,16,128]{3,2,0,1:T(8,128)}), f32[1,256,16,128]{3,2,0,1:T(8,128)}, u32[]{:S(2)}, u32[]{:S(2)}) %all-to-all-start.1) | async-done | bytes 2097184 | tf_op jit(solution)/shard_map/all_to_all | solution.py:114
  265.4 2.9 collective-permute-done
  269.8 6.0 %collective-permute-done.1 = bf16[64,2048]{1,0:T(8,128)(2,1)S(1)} collective-permute-done((bf16[64,2048]{1,0:T(8,128)(2,1)S(1)}, bf16[64,2048]{1,0:T(8,128)(2,1)S(1)}, u32[]{:S(2)}, u32[]{:S(2)}) %collective-permute-start.1) | collective-permute-done | bytes 262176 | tf_op jit(solution)/shard_map/ppermute | solution.py:15
  276.3 23.8 %collective-permute-done.2 = bf16[128,2048]{1,0:T(8,128)(2,1)S(1)} collective-permute-done((bf16[128,2048]{1,0:T(8,128)(2,1)S(1)}, bf16[128,2048]{1,0:T(8,128)(2,1)S(1)}, u32[]{:S(2)}, u32[]{:S(2)}) %collective-permute-start.2) | collective-permute-done | bytes 524320 | tf_op jit(solution)/shard_map/ppermute | solution.py:15
  302.7 26.9 %reduce-scatter.2.cloned.1.call-done = f32[64,1024]{1,0:T(8,128)} async-done(((f32[256,1024]{1,0:T(8,128)}), f32[64,1024]{1,0:T(8,128)}) %reduce-scatter.2.cloned.1.call-update) | async-done | bytes 262160 | tf_op jit(solution)/shard_map/reduce_scatter | solution.py:132
  (89 shorter events, 32.7 us)
Async XLA Ops:
  6.5 1.5 copy-start
  134.0 4.1 %copy-start.1 = (f32[2,8,256,128]{3,2,1,0:T(8,128)S(1)}, f32[2,8,256,128]{3,2,1,0:T(8,128)}, u32[]{:S(2)}) copy-start(f32[2,8,256,128]{3,2,1,0:T(8,128)} %get-tuple-element.276) | copy-start | bytes 6291460 | tf_op jit(solution)/shard_map/while
  144.8 1.3 copy-start.2
  150.6 4.1 %copy-start.1 = (f32[2,8,256,128]{3,2,1,0:T(8,128)S(1)}, f32[2,8,256,128]{3,2,1,0:T(8,128)}, u32[]{:S(2)}) copy-start(f32[2,8,256,128]{3,2,1,0:T(8,128)} %get-tuple-element.276) | copy-start | bytes 6291460 | tf_op jit(solution)/shard_map/while
  161.4 1.3 copy-start.2
  167.2 4.1 %copy-start.1 = (f32[2,8,256,128]{3,2,1,0:T(8,128)S(1)}, f32[2,8,256,128]{3,2,1,0:T(8,128)}, u32[]{:S(2)}) copy-start(f32[2,8,256,128]{3,2,1,0:T(8,128)} %get-tuple-element.276) | copy-start | bytes 6291460 | tf_op jit(solution)/shard_map/while
  178.0 1.3 copy-start.2
  183.8 4.1 %copy-start.1 = (f32[2,8,256,128]{3,2,1,0:T(8,128)S(1)}, f32[2,8,256,128]{3,2,1,0:T(8,128)}, u32[]{:S(2)}) copy-start(f32[2,8,256,128]{3,2,1,0:T(8,128)} %get-tuple-element.276) | copy-start | bytes 6291460 | tf_op jit(solution)/shard_map/while
  194.6 1.3 copy-start.2
  198.2 10.1 %all-to-all-start = ((f32[8,1,512]{2,1,0:T(1,128)}), f32[8,1,512]{2,1,0:T(1,128)S(1)}, u32[]{:S(2)}, u32[]{:S(2)}) async-start(f32[8,1,512]{2,1,0:T(1,128)} %reshape.106), calls=%async_computation | async-start | bytes 32768 | tf_op jit(solution)/shard_map/all_to_all | solution.py:113
  208.3 4.8 %copy-start.3 = (s32[256]{0:T(256)S(1)}, s32[256]{0:T(256)}, u32[]{:S(2)}) copy-start(s32[256]{0:T(256)} %param.15) | copy-start | bytes 3076
  208.3 51.5 %all-to-all-start.1 = ((f32[1,256,16,128]{3,2,0,1:T(8,128)}), f32[1,256,16,128]{3,2,0,1:T(8,128)}, u32[]{:S(2)}, u32[]{:S(2)}) async-start(f32[1,256,16,128]{3,2,0,1:T(8,128)} %bitcast.114), calls=%async_computation.1 | async-start | bytes 4194304 | tf_op jit(solution)/shard_map/all_to_all | solution.py:114
  212.7 116.9 %reduce-scatter.2.cloned.1.call-start = ((), (), s32[]{:S(2)}) async-start(), calls=%async_computation.3 | async-start | bytes 1310720 | tf_op jit(solution)/shard_map/reduce_scatter | solution.py:132
  263.0 5.4 %collective-permute-start = (bf16[32,2048]{1,0:T(8,128)(2,1)S(1)}, bf16[32,2048]{1,0:T(8,128)(2,1)S(1)}, u32[]{:S(2)}, u32[]{:S(2)}) collective-permute-start(bf16[32,2048]{1,0:T(8,128)(2,1)S(1)} %copy_bitcast_fusion.1), channel_id=1, source_target_pairs={{0,28},{4,0},{8,4},{12,8},{16,12},{20,16},{24,20},{28,24},{1,29},{... | collective-permute-start | bytes 393224 | tf_op jit(solution)/shard_map/ppermute | solution.py:15
  268.4 7.4 %collective-permute-start.1 = (bf16[64,2048]{1,0:T(8,128)(2,1)S(1)}, bf16[64,2048]{1,0:T(8,128)(2,1)S(1)}, u32[]{:S(2)}, u32[]{:S(2)}) collective-permute-start(bf16[64,2048]{1,0:T(8,128)(2,1)S(1)} %pad_maximum_fusion.1), channel_id=1, source_target_pairs={{0,24},{4,28},{8,0},{12,4},{16,8},{20,12},{24,16},{28,20},{1,25},{... | collective-permute-start | bytes 786440 | tf_op jit(solution)/shard_map/ppermute | solution.py:15
  275.8 24.3 %collective-permute-start.2 = (bf16[128,2048]{1,0:T(8,128)(2,1)S(1)}, bf16[128,2048]{1,0:T(8,128)(2,1)S(1)}, u32[]{:S(2)}, u32[]{:S(2)}) collective-permute-start(bf16[128,2048]{1,0:T(8,128)(2,1)S(1)} %pad_maximum_fusion), channel_id=1, source_target_pairs={{0,16},{4,20},{8,24},{12,28},{16,0},{20,4},{24,8},{28,12},{1,17},{... | collective-permute-start | bytes 1572872 | tf_op jit(solution)/shard_map/ppermute | solution.py:15
  276.1 24.3 %copy-start.4 = (bf16[2048,1024]{1,0:T(8,128)(2,1)S(1)}, bf16[2048,1024]{1,0:T(8,128)(2,1)}, u32[]{:S(2)}) copy-start(bf16[2048,1024]{1,0:T(8,128)(2,1)} %param.12) | copy-start | bytes 12582916
Sparse Core Ops, SparseCore 0:
  302.8 26.7 reduce-scatter.1
